TPU v7x, 32 devices: a whole 2x2x4 slice. The times are simulated.
32 devices in a mesh: sub: 8 (over z, x), load: 4 (over y, core).
Axes of the slice: x: 2, y: 2, z: 4, core: 2. Of those that a mesh axis runs over, the one named last changes fastest.
Arguments:
- dual_ops: bfloat16 [32, 1024, 1024], P(('sub', 'load')), may hold values from -0.1875 to 0.1875
- dual_rhs: float32 [32, 1024, 128], P(('sub', 'load')), may hold values from -6 to 6
- partner: int32 [32, 1024], P(('sub', 'load')), may hold values from 0 to 3071, as said below
- coarse_basis: bfloat16 [32, 12, 1024], P(('sub', 'load')), may hold values from -0.1875 to 0.1875
- coarse_inverse: float32 [384, 384], P(('sub', 'load')), as said below
- damping: float32 [128], replicated, may hold values from 0.05 to 0.5
- recovery: bfloat16 [32, 1536, 1024], P(('sub', 'load')), may hold values from -0.1875 to 0.1875
- base_disp: bfloat16 [32, 1536, 128], P(('sub', 'load')), may hold values from -6 to 6
- adjoint: bfloat16 [32, 1536, 128], P(('sub', 'load')), may hold values from -6 to 6
- elem_voxel: int32 [32, 128], P(('sub', 'load')), may hold values from 0 to 8191
- fibre_class: int32 [64, 512], P('sub', 'load'), may hold values from 0 to 3
Outputs:
- multipliers: float32 [32, 1024, 128], P(('sub', 'load'))
- gradient_field: float32 [64, 512], P('sub', 'load')
Inputs may be any that keep to these rules, and one draw needn't show every extreme that they name: `partner`: entry (s, j) names the other copy of the same multiplier among the subdomains s - 1 (values 0 to 1023), s (1024 to 2047) and s + 1 (2048 to 3071), wrapping around over all 32 subdomains, as v mod 1024 = the copy's row. The pairing is one to one and symmetric; in every subdomain a quarter of the entries point to s - 1, a quarter to s + 1 and half inside. `elem_voxel`: value v places the element at grid row v // 128 and at column v mod 128 of the 128 columns of its subdomain's block of columns. coarse_inverse equals its transpose.
All inputs are finite; a program needn't handle non-finite values.
Results may differ from a plain program's by a relative error of at most 0.0021.
Values may be sent and summed in bfloat16 or wider, within the bound.
A program may use at most 64 MiB of HBM per device.

v0:
```python
import functools
import math

import jax
import jax.numpy as jnp
from jax import lax
from jax.experimental import pallas as pl
from jax.experimental.pallas import tpu as pltpu
from jax.sharding import PartitionSpec as P

EDOF = 12
ITERS = 3
SMOOTH = 2
FIBRE_RATE = 0.3
ISO_RATE = 0.05
EPSILON = 1e-06

F32 = jnp.float32
BF16 = jnp.bfloat16
I32 = jnp.int32
MESH = pl.DeviceIdType.MESH
LANES = 128
CHUNK = 256
RP = 16
GROUP = 32
MARGIN_R = 4
MARGIN_C = 64


def iota(shape, dim):
    return lax.broadcasted_iota(I32, shape, dim)


def hot(cond):
    return jnp.where(cond, 1.0, 0.0).astype(BF16)


def split(value):
    high = value.astype(BF16)
    return high, (value - high.astype(F32)).astype(BF16)


def kernel(
    ns, nl,
    a_h, rhs_h, par_h, b_h, ci_h, damp_h, rec_h, base_h, adj_h, ev_h, fc_h,
    x_h, f_h,
    a, rhs, par, b, ci, damp, rec, base, adj, evb, fcb,
    own_hot, recv_hot, send_hot, x, xb, img, tmp, res, parts, snd, rcv,
    bwide, bt, bp, spread, cpf, cp, ag, ck, prod, sel, egb, colhot, rowval, fout,
    lsem, nsend, nrecv, gsend, grecv, vsend, vrecv, csend, crecv, esend, erecv,
):
    n = ns * nl
    spots = a.shape[0]
    quarter = spots // 4
    modes = b.shape[0]
    sub, load = lax.axis_index("sub"), lax.axis_index("load")
    me = sub * nl + load

    def dev(p):
        return (lax.div(p, nl), lax.rem(p, nl))

    def peer(k):
        return lax.rem(me + k, n)

    local = [
        pltpu.make_async_copy(src, dst, lsem.at[i])
        for i, (src, dst) in enumerate((
            (par_h, par),
            (b_h.at[0], b),
            (ci_h, ci),
            (ev_h, evb.at[me]),
            (fc_h, fcb.at[4]),
            (damp_h, damp),
            (a_h.at[0], a),
            (rhs_h.at[0], rhs),
            (rec_h.at[0], rec),
            (base_h.at[0], base),
            (adj_h.at[0], adj),
        ))
    ]
    for copy in local[:8]:
        copy.start()

    barrier = pltpu.get_barrier_semaphore()

    def each_peer(act):
        @pl.loop(0, ns)
        def _(i):
            far = jnp.where(2 * sub < ns, ns - 1 - i, i)
            for j in range(nl):
                across = jnp.where(2 * load < nl, nl - 1 - j, j)

                @pl.when(far * nl + across != me)
                def _():
                    act((far, across))

    each_peer(lambda to: pl.semaphore_signal(barrier, inc=1, device_id=to, device_id_type=MESH))

    local[0].wait()
    prow = par[...].astype(F32)
    lane = iota((LANES, LANES), 1).astype(F32)
    blocks = spots // LANES
    for r in range(blocks):
        rows = pl.ds(r * LANES, LANES)
        pcol = jnp.transpose(jnp.broadcast_to(prow[:, r * LANES:(r + 1) * LANES], (LANES, LANES)))
        below = jnp.zeros((LANES, LANES), F32)
        for c in range(blocks):
            cols = pl.ds(c * LANES, LANES)
            own_hot[rows, cols] = hot(pcol == lane + float(spots + c * LANES))
            below = below + jnp.where(pcol > prow[:, c * LANES:(c + 1) * LANES], 1.0, 0.0)
        rank = jnp.broadcast_to(jnp.sum(below, axis=1, keepdims=True), (LANES, LANES))
        place = jnp.where(
            pcol < float(spots),
            rank,
            jnp.where(pcol >= float(2 * spots), rank - float(2 * quarter), -1.0),
        )
        for c in range(2 * quarter // LANES):
            recv_hot[rows, pl.ds(c * LANES, LANES)] = hot(place == lane + float(c * LANES))
    to_next = jnp.where(prow >= float(2 * spots), 1.0, 0.0)
    to_prev = jnp.where(prow < float(spots), 1.0, 0.0)
    count = jnp.where(iota((8, spots), 0) == 0, to_next, to_prev)
    wide = iota((8, spots), 1)
    shift = 1
    while shift < spots:
        count = count + jnp.where(wide >= shift, pltpu.roll(count, shift, 1), 0.0)
        shift *= 2
    slot = jnp.where(
        to_next > 0.5,
        count[0:1] - 1.0,
        jnp.where(to_prev > 0.5, count[1:2] - 1.0 + float(quarter), -1.0),
    )
    for r in range(2 * quarter // LANES):
        at = (iota((LANES, spots), 0) + r * LANES).astype(F32)
        send_hot[pl.ds(r * LANES, LANES), :] = hot(slot == at)

    local[1].wait()
    bwide[...] = jnp.zeros_like(bwide)
    basis = b[...].astype(F32)
    bwide[0:modes, :] = basis
    bwide[RP:RP + modes, :] = basis
    bp[...] = bwide[0:RP, :].astype(BF16)
    for r in range(blocks):
        bt[pl.ds(r * LANES, LANES), :] = jnp.transpose(
            bwide[:, r * LANES:(r + 1) * LANES]
        ).astype(BF16)
    ck[...] = jnp.zeros_like(ck)
    local[2].wait()
    deep, broad = spread.shape
    at_col = iota((deep, broad), 1)
    within = at_col & (RP - 1)
    from_row = (at_col >> 4) * modes + within
    spread[...] = hot((iota((deep, broad), 0) == from_row) & (within < modes))
    cpf[...] = jnp.zeros_like(cpf)
    for g in range(n // GROUP):
        high, rest = split(ci[:, g * deep:(g + 1) * deep])
        cols = pl.ds(g * broad, broad)
        cpf[0:modes, cols] = jnp.dot(high, spread[...], preferred_element_type=F32)
        cpf[RP:RP + modes, cols] = jnp.dot(rest, spread[...], preferred_element_type=F32)
        mode = iota((1, broad), 1) & (RP - 1)
        cpf[modes:modes + 1, cols] = jnp.where((mode == modes) | (mode == modes + 1), 1.0, 0.0)
    cp[...] = cpf[...].astype(BF16)
    offset = iota(sel.shape, 1) - EDOF * iota(sel.shape, 0)
    sel[...] = hot((offset >= 0) & (offset < EDOF))
    x[...] = jnp.zeros_like(x)
    xb[...] = jnp.zeros_like(xb)

    local[3].wait()
    local[4].wait()
    local[5].wait()
    def to_all(ref, send, recv):
        each_peer(lambda to: pltpu.make_async_remote_copy(
            src_ref=ref.at[me], dst_ref=ref.at[me], send_sem=send, recv_sem=recv,
            device_id=to, device_id_type=MESH,
        ).start())

    def settle(ref, sem):
        part = ref.at[pl.ds(0, n - 1)]
        pltpu.make_async_copy(part, part, sem).wait()

    local[6].wait()
    local[7].wait()
    for copy in local[8:]:
        copy.start()

    entries = float(n * spots)
    near = []
    for it in range(ITERS):
        @pl.loop(0, spots // CHUNK, unroll=True)
        def _(r):
            rows = pl.ds(pl.multiple_of(r * CHUNK, CHUNK), CHUNK)
            img[rows, :] = jnp.dot(a[rows, :], xb[...], preferred_element_type=F32).astype(BF16)

        snd[it] = jnp.dot(send_hot[...], img[...], preferred_element_type=F32).astype(BF16)
        if it == 0:
            pl.semaphore_wait(barrier, n - 1)
        for side, step in enumerate((1, n - 1)):
            half = pl.ds(side * quarter, quarter)
            copy = pltpu.make_async_remote_copy(
                src_ref=snd.at[it, half], dst_ref=rcv.at[it, half],
                send_sem=nsend.at[it, side], recv_sem=nrecv.at[it, side],
                device_id=dev(peer(step)), device_id_type=MESH,
            )
            copy.start()
            near.append(copy)

        @pl.loop(0, spots // CHUNK, unroll=True)
        def _(r):
            rows = pl.ds(pl.multiple_of(r * CHUNK, CHUNK), CHUNK)
            tmp[rows, :] = img[rows, :].astype(F32) + jnp.dot(
                own_hot[rows, :], img[...], preferred_element_type=F32
            )

        near[-2].wait_recv()
        near[-1].wait_recv()

        def residual(r, total):
            rows = pl.ds(pl.multiple_of(r * CHUNK, CHUNK), CHUNK)
            left = rhs[rows, :] - (
                tmp[rows, :] + jnp.dot(recv_hot[rows, :], rcv[it], preferred_element_type=F32)
            )
            res[rows, :] = left
            high, rest = split(left)
            parts[rows, 0:LANES] = high
            parts[rows, LANES:2 * LANES] = rest
            return total + jnp.sum((left * left).reshape(CHUNK // 8, 8, LANES), axis=0)

        total = lax.fori_loop(
            0, spots // CHUNK, residual, jnp.zeros((8, LANES), F32), unroll=True
        )
        both = jnp.dot(bp[...], parts[...], preferred_element_type=F32)
        terms = both[:, 0:LANES] + both[:, LANES:2 * LANES]
        squares = jnp.sum(total, axis=0, keepdims=True)
        high, rest = split(squares)
        row = iota((RP, LANES), 0)
        terms = jnp.where(row == modes, high.astype(F32), terms)
        terms = jnp.where(row == modes + 1, rest.astype(F32), terms)
        ag[it, me] = terms.astype(BF16)
        to_all(ag.at[it], gsend.at[it], grecv.at[it])

        if it == 0:
            to_all(evb, vsend, vrecv)
            around = [(i, j) for i in (-1, 0, 1) for j in (-1, 0, 1) if (i, j) != (0, 0)]
            for i, j in around:
                pltpu.make_async_remote_copy(
                    src_ref=fcb.at[4], dst_ref=fcb.at[(1 - i) * 3 + 1 - j],
                    send_sem=csend, recv_sem=crecv,
                    device_id=(lax.rem(sub + i + ns, ns), lax.rem(load + j + nl, nl)),
                    device_id_type=MESH,
                ).start()
        if it == 1:
            settle(evb, vrecv)

            @pl.loop(0, n)
            def _(s):
                column = evb[s] & (LANES - 1)
                spot = (lax.rem(s, nl) - load) * LANES + column + MARGIN_C
                colhot[:, pl.ds(pl.multiple_of(s * LANES, LANES), LANES)] = hot(
                    iota((2 * LANES, LANES), 0) == spot
                )

        settle(ag.at[it], grecv.at[it])
        solved = jnp.dot(
            cp[...], ag[it].reshape(n * RP, LANES), preferred_element_type=F32
        )
        correction = solved[0:RP] + solved[RP:2 * RP]
        mean = correction[modes:modes + 1] / entries
        step_size = damp[...] / jnp.sqrt(mean + EPSILON)
        high, rest = split(correction)
        ck[0:RP, :] = high
        ck[RP:2 * RP, :] = rest

        @pl.loop(0, spots // CHUNK, unroll=True)
        def _(r):
            rows = pl.ds(pl.multiple_of(r * CHUNK, CHUNK), CHUNK)
            projected = res[rows, :] - jnp.dot(bt[rows, :], ck[...], preferred_element_type=F32)
            new = x[rows, :] + step_size * projected
            x[rows, :] = new
            xb[rows, :] = new.astype(BF16)

    out_copy = pltpu.make_async_copy(x, x_h.at[0], lsem.at[11])
    out_copy.start()
    for copy in local[8:]:
        copy.wait()
    unknowns = rec.shape[0]

    @pl.loop(0, unknowns // CHUNK, unroll=True)
    def _(r):
        rows = pl.ds(pl.multiple_of(r * CHUNK, CHUNK), CHUNK)
        displaced = base[rows, :].astype(F32) - jnp.dot(
            rec[rows, :], xb[...], preferred_element_type=F32
        )
        high, rest = split(displaced * adj[rows, :].astype(F32))
        prod[rows, 0:LANES] = high
        prod[rows, LANES:2 * LANES] = rest

    both = jnp.dot(sel[...], prod[...], preferred_element_type=F32)
    grads = jnp.sum(
        jnp.transpose(both[:, 0:LANES] + both[:, LANES:2 * LANES]), axis=0, keepdims=True
    ) / math.sqrt(EDOF * LANES)
    egb[me] = grads
    to_all(egb, esend, erecv)

    pltpu.make_async_copy(fcb.at[pl.ds(0, 8)], fcb.at[pl.ds(0, 8)], crecv).wait()
    classes = jnp.concatenate(
        [jnp.concatenate([fcb[3 * i + j] for j in range(3)], axis=1) for i in range(3)], axis=0
    )
    high_r, wide_c = 2 * 8, 2 * LANES
    classes = pltpu.roll(classes, 3 * 8 - (8 - MARGIN_R), 0)[0:high_r]
    classes = pltpu.roll(classes, 3 * LANES - (LANES - MARGIN_C), 1)[:, 0:wide_c]
    grid_row = iota((high_r, wide_c), 0) + (sub * 8 - MARGIN_R)
    grid_col = iota((high_r, wide_c), 1) + (load * LANES - MARGIN_C)
    inside = (grid_row >= 0) & (grid_row < ns * 8) & (grid_col >= 0) & (grid_col < nl * LANES)

    settle(egb, erecv)

    def place_rows(s, carry):
        here = iota((RP, LANES), 0) == (evb[s] >> 7) - (sub * 8 - MARGIN_R)
        high, rest = split(jnp.where(here, egb[s], 0.0))
        cols = pl.ds(pl.multiple_of(s * LANES, LANES), LANES)
        rowval[0:RP, cols] = high
        rowval[RP:2 * RP, cols] = rest
        return carry

    lax.fori_loop(0, n, place_rows, 0, unroll=8)
    sums = lax.dot_general(
        rowval[...], colhot[...], (((1,), (1,)), ((), ())), preferred_element_type=F32
    )
    field = sums[0:RP] + sums[RP:2 * RP]

    def moved(value, by_row, by_col):
        if by_row:
            value = pltpu.roll(value, (-by_row) % high_r, 0)
        if by_col:
            value = pltpu.roll(value, (-by_col) % wide_c, 1)
        return value

    for repeat in range(SMOOTH):
        field = jnp.where(inside, field, 0.0)
        up, down = moved(field, 1, 0), moved(field, -1, 0)
        along_rows = up + down - 2.0 * field
        along_cols = moved(field, 0, 1) + moved(field, 0, -1) - 2.0 * field
        diag_main = moved(up, 0, 1) + moved(down, 0, -1) - 2.0 * field
        diag_anti = moved(up, 0, -1) + moved(down, 0, 1) - 2.0 * field
        chosen = jnp.where(
            classes == 0,
            along_rows,
            jnp.where(classes == 1, along_cols, jnp.where(classes == 2, diag_main, diag_anti)),
        )
        field = field + FIBRE_RATE * chosen + ISO_RATE * (along_rows + along_cols)
    fout[...] = moved(field, MARGIN_R, MARGIN_C)[0:8, 0:LANES]
    field_copy = pltpu.make_async_copy(fout, f_h, lsem.at[12])
    field_copy.start()

    for copy in near:
        copy.wait_send()
    for it in range(ITERS):
        settle(ag.at[it], gsend.at[it])
    settle(evb, vsend)
    settle(egb, esend)
    pltpu.make_async_copy(fcb.at[pl.ds(0, 8)], fcb.at[pl.ds(0, 8)], csend).wait()
    out_copy.wait()
    field_copy.wait()


def on_device(ns, nl, *args):
    (dual_ops, dual_rhs, partner, coarse_basis, coarse_inverse, damping,
     recovery, base_disp, adjoint, elem_voxel, fibre_class) = args
    n = ns * nl
    spots, columns = dual_rhs.shape[1:]
    modes = coarse_basis.shape[1]
    unknowns = recovery.shape[1]
    elements = elem_voxel.shape[1]
    half = spots // 2
    dma = pltpu.SemaphoreType.DMA
    scratch = [
        pltpu.VMEM((spots, spots), BF16),
        pltpu.VMEM((spots, columns), F32),
        pltpu.VMEM((1, spots), I32),
        pltpu.VMEM((modes, spots), BF16),
        pltpu.VMEM(coarse_inverse.shape, F32),
        pltpu.VMEM((1, columns), F32),
        pltpu.VMEM((unknowns, spots), BF16),
        pltpu.VMEM((unknowns, columns), BF16),
        pltpu.VMEM((unknowns, columns), BF16),
        pltpu.VMEM((n, 1, elements), I32),
        pltpu.VMEM((9,) + fibre_class.shape, I32),
        pltpu.VMEM((spots, spots), BF16),
        pltpu.VMEM((spots, half), BF16),
        pltpu.VMEM((half, spots), BF16),
        pltpu.VMEM((spots, columns), F32),
        pltpu.VMEM((spots, columns), BF16),
        pltpu.VMEM((spots, columns), BF16),
        pltpu.VMEM((spots, columns), F32),
        pltpu.VMEM((spots, columns), F32),
        pltpu.VMEM((spots, 2 * columns), BF16),
        pltpu.VMEM((ITERS, half, columns), BF16),
        pltpu.VMEM((ITERS, half, columns), BF16),
        pltpu.VMEM((LANES, spots), F32),
        pltpu.VMEM((spots, LANES), BF16),
        pltpu.VMEM((RP, spots), BF16),
        pltpu.VMEM((GROUP * modes, GROUP * RP), BF16),
        pltpu.VMEM((2 * RP, n * RP), F32),
        pltpu.VMEM((2 * RP, n * RP), BF16),
        pltpu.VMEM((ITERS, n, RP, columns), BF16),
        pltpu.VMEM((LANES, columns), BF16),
        pltpu.VMEM((unknowns, 2 * columns), BF16),
        pltpu.VMEM((elements, unknowns), BF16),
        pltpu.VMEM((n, 1, elements), F32),
        pltpu.VMEM((2 * LANES, n * elements), BF16),
        pltpu.VMEM((2 * RP, n * elements), BF16),
        pltpu.VMEM(fibre_class.shape, F32),
        dma((13,)),
        dma((ITERS, 2)),
        dma((ITERS, 2)),
        dma((ITERS,)),
        dma((ITERS,)),
        dma, dma, dma, dma, dma, dma,
    ]
    anywhere = pl.BlockSpec(memory_space=pl.ANY)
    multipliers, field = pl.pallas_call(
        functools.partial(kernel, ns, nl),
        out_shape=(
            jax.ShapeDtypeStruct((1, spots, columns), F32),
            jax.ShapeDtypeStruct(fibre_class.shape, F32),
        ),
        in_specs=[anywhere] * 11,
        out_specs=(anywhere, anywhere),
        scratch_shapes=scratch,
        compiler_params=pltpu.CompilerParams(
            collective_id=0, has_side_effects=True, vmem_limit_bytes=62 * 1024 * 1024
        ),
    )(
        dual_ops, dual_rhs, partner, coarse_basis, coarse_inverse,
        damping.reshape(1, columns), recovery, base_disp, adjoint, elem_voxel, fibre_class,
    )
    return multipliers, field


def solution(mesh):
    ns, nl = mesh.shape["sub"], mesh.shape["load"]
    placed = (
        P(("sub", "load"), None, None),
        P(("sub", "load"), None, None),
        P(("sub", "load"), None),
        P(("sub", "load"), None, None),
        P(("sub", "load"), None),
        P(),
        P(("sub", "load"), None, None),
        P(("sub", "load"), None, None),
        P(("sub", "load"), None, None),
        P(("sub", "load"), None),
        P("sub", "load"),
    )
    return jax.shard_map(
        functools.partial(on_device, ns, nl),
        mesh=mesh,
        in_specs=placed,
        out_specs=(P(("sub", "load"), None, None), P("sub", "load")),
        check_vma=False,
    )
```

profile of v0, /device:TPU:0, one launch (start us, length us, event | category | flops | bytes accessed | tf_op | source)
XLA Modules:
  0.0 51.4 jit_solution(5666908052177197014)
XLA Ops:
  0.6 47.6 %shard_map.122 = (f32[1,1024,128]{2,1,0:T(8,128)}, f32[8,128]{1,0:T(8,128)}) custom-call(bf16[1,1024,1024]{2,1,0:T(8,128)(2,1)} %a_h.1, f32[1,1024,128]{2,1,0:T(8,128)} %rhs_h.1, s32[1,1024]{1,0:T(1,128)} %par_h.1, bf16[1,12,1024]{2,1,0:T(8,128)(2,1)} %b_h.1, f32[12,384]{1,0:T(8,128)} %ci_h.1, f32[1,128]{1,0:T(1,128)} %bitcast.1, ...), custom_call_target="tpu_custom_call" | custom-call | tf_op jit(solution)/shard_map/pallas_call | solution.py:420
  48.3 1.9 %copy.15 = f32[1,1024,128]{2,1,0:T(8,128)} copy(f32[1,1024,128]{2,1,0:T(8,128)} %get-tuple-element.4) | data formatting | bytes 1048576
  50.1 1.3 %copy.16 = f32[8,128]{1,0:T(8,128)} copy(f32[8,128]{1,0:T(8,128)} %get-tuple-element.5) | data formatting | bytes 8192
where the time goes:
time: 51.6 us; the launch traced here: 51.4 us
  Pallas kernels  47.6 us (92%)
  local copies, waits for them, and re-layouts  3.13 us (6%)
  between operations  0.64 us (1%)
    pallas_call x1, Pallas kernels, on_device(): pl.pallas_call(functools.partial(kernel, ns, nl), out_shape=(jax.ShapeDty...  47.6 us
    unnamed x2, local copies, waits for them, and re-layouts  3.13 us

commit v1 on v0

v1 whole, which is shorter than its diff:
```python
import functools
import math

import jax
import jax.numpy as jnp
from jax import lax
from jax.experimental import pallas as pl
from jax.experimental.pallas import tpu as pltpu
from jax.sharding import PartitionSpec as P

EDOF = 12
ITERS = 3
SMOOTH = 2
FIBRE_RATE = 0.3
ISO_RATE = 0.05
EPSILON = 1e-06

F32 = jnp.float32
BF16 = jnp.bfloat16
I32 = jnp.int32
MESH = pl.DeviceIdType.MESH
LANES = 128
CHUNK = 256
RP = 16
GROUP = 32
MARGIN_R = 4
MARGIN_C = 64


def iota(shape, dim):
    return lax.broadcasted_iota(I32, shape, dim)


def hot(cond):
    return jnp.where(cond, 1.0, 0.0).astype(BF16)


def split(value):
    high = value.astype(BF16)
    return high, (value - high.astype(F32)).astype(BF16)


def kernel(
    ns, nl,
    a_h, rhs_h, par_h, b_h, ci_h, damp_h, rec_h, base_h, adj_h, ev_h, fc_h,
    x_h, f_h,
    a, rhs, par, b, ci, damp, rec, base, adj, evb, fcb,
    own_hot, recv_hot, send_hot, x, xr, img, y, res, parts, snd, rcv, snd1, rcv1,
    bwide, bt, bp, spread, cpf, cp, ag, ck, hw, ckw, rb, da, db,
    prod, sel, egb, colhot, rowval, fout,
    lsem, nsend, nrecv, gsend, grecv, psend, precv, vsend, vrecv, csend, crecv, esend, erecv,
):
    n = ns * nl
    spots = a.shape[0]
    quarter = spots // 4
    modes = b.shape[0]
    sub, load = lax.axis_index("sub"), lax.axis_index("load")
    me = sub * nl + load

    def dev(p):
        return (lax.div(p, nl), lax.rem(p, nl))

    def peer(k):
        return lax.rem(me + k, n)

    local = [
        pltpu.make_async_copy(src, dst, lsem.at[i])
        for i, (src, dst) in enumerate((
            (b_h.at[0], b),
            (rhs_h.at[0], rhs),
            (par_h, par),
            (ci_h, ci),
            (damp_h, damp),
            (a_h.at[0], a),
            (ev_h, evb.at[me]),
            (fc_h, fcb.at[4]),
            (rec_h.at[0], rec),
            (base_h.at[0], base),
            (adj_h.at[0], adj),
        ))
    ]
    for copy in local[:8]:
        copy.start()

    barrier = pltpu.get_barrier_semaphore()

    def each_peer(act):
        @pl.loop(0, ns)
        def _(i):
            far = jnp.where(2 * sub < ns, ns - 1 - i, i)
            for j in range(nl):
                across = jnp.where(2 * load < nl, nl - 1 - j, j)

                @pl.when(far * nl + across != me)
                def _():
                    act((far, across))

    each_peer(lambda to: pl.semaphore_signal(barrier, inc=1, device_id=to, device_id_type=MESH))

    def to_all(ref, send, recv):
        each_peer(lambda to: pltpu.make_async_remote_copy(
            src_ref=ref.at[me], dst_ref=ref.at[me], send_sem=send, recv_sem=recv,
            device_id=to, device_id_type=MESH,
        ).start())

    def settle(ref, sem):
        part = ref.at[pl.ds(0, n - 1)]
        pltpu.make_async_copy(part, part, sem).wait()

    def chunk(r):
        return pl.ds(r * CHUNK, CHUNK)

    chunks = spots // CHUNK

    def gather_terms(it, total):
        both = jnp.dot(bp[...], parts[...], preferred_element_type=F32)
        terms = both[:, 0:LANES] + both[:, LANES:2 * LANES]
        squares = jnp.sum(total, axis=0, keepdims=True)
        high, rest = split(squares)
        row = iota((RP, LANES), 0)
        terms = jnp.where(row == modes, high.astype(F32), terms)
        terms = jnp.where(row == modes + 1, rest.astype(F32), terms)
        ag[it, me] = terms.astype(BF16)

    def keep_parts(rows, left):
        high, rest = split(left)
        parts[rows, 0:LANES] = high
        parts[rows, LANES:2 * LANES] = rest
        return jnp.sum((left * left).reshape(CHUNK // 8, 8, LANES), axis=0)

    blocks = spots // LANES
    local[0].wait()
    bwide[...] = jnp.zeros_like(bwide)
    basis = b[...].astype(F32)
    for d in range(4):
        bwide[d * RP:d * RP + modes, :] = basis
    bp[...] = bwide[0:RP, :].astype(BF16)
    local[1].wait()
    total = jnp.zeros((8, LANES), F32)
    for r in range(chunks):
        total = total + keep_parts(chunk(r), rhs[chunk(r), :])
    gather_terms(0, total)

    for r in range(blocks):
        bt[pl.ds(r * LANES, LANES), :] = jnp.transpose(
            bwide[:, r * LANES:(r + 1) * LANES]
        ).astype(BF16)
    ck[...] = jnp.zeros_like(ck)
    ckw[...] = jnp.zeros_like(ckw)
    local[3].wait()
    deep, broad = spread.shape
    at_col = iota((deep, broad), 1)
    within = at_col & (RP - 1)
    from_row = (at_col >> 4) * modes + within
    spread[...] = hot((iota((deep, broad), 0) == from_row) & (within < modes))
    cpf[...] = jnp.zeros_like(cpf)
    for g in range(n // GROUP):
        high, rest = split(ci[:, g * deep:(g + 1) * deep])
        cols = pl.ds(g * broad, broad)
        cpf[0:modes, cols] = jnp.dot(high, spread[...], preferred_element_type=F32)
        cpf[RP:RP + modes, cols] = jnp.dot(rest, spread[...], preferred_element_type=F32)
        mode = iota((1, broad), 1) & (RP - 1)
        cpf[modes:modes + 1, cols] = jnp.where((mode == modes) | (mode == modes + 1), 1.0, 0.0)
    own_cp = pl.ds(4 * RP, 2 * RP)
    cp[own_cp, :] = cpf[...].astype(BF16)

    local[2].wait()
    prow = par[...].astype(F32)
    to_next = jnp.where(prow >= float(2 * spots), 1.0, 0.0)
    to_prev = jnp.where(prow < float(spots), 1.0, 0.0)
    count = jnp.where(iota((8, spots), 0) == 0, to_next, to_prev)
    wide = iota((8, spots), 1)
    shift = 1
    while shift < spots:
        count = count + jnp.where(wide >= shift, pltpu.roll(count, shift, 1), 0.0)
        shift *= 2
    slot = jnp.where(
        to_next > 0.5,
        count[0:1] - 1.0,
        jnp.where(to_prev > 0.5, count[1:2] - 1.0 + float(quarter), -1.0),
    )
    for r in range(2 * quarter // LANES):
        at = (iota((LANES, spots), 0) + r * LANES).astype(F32)
        send_hot[pl.ds(r * LANES, LANES), :] = hot(slot == at)

    for i in (4, 5, 6, 7):
        local[i].wait()
    for copy in local[8:]:
        copy.start()

    pl.semaphore_wait(barrier, n - 1)
    to_all(ag.at[0], gsend.at[0], grecv.at[0])
    near = []
    for side, step in enumerate((1, n - 1)):
        copy = pltpu.make_async_remote_copy(
            src_ref=cp.at[own_cp], dst_ref=cp.at[pl.ds(side * 2 * RP, 2 * RP)],
            send_sem=psend.at[side], recv_sem=precv.at[side],
            device_id=dev(peer(step)), device_id_type=MESH,
        )
        copy.start()
        near.append(copy)

    def exchange(it):
        copies = []
        for side, step in enumerate((1, n - 1)):
            half = pl.ds(side * quarter, quarter)
            src, dst = (snd, rcv) if it == 0 else (snd1, rcv1)
            copy = pltpu.make_async_remote_copy(
                src_ref=src.at[half], dst_ref=dst.at[half],
                send_sem=nsend.at[it, side], recv_sem=nrecv.at[it, side],
                device_id=dev(peer(step)), device_id_type=MESH,
            )
            copy.start()
            copies.append(copy)
        return copies

    for r in range(chunks):
        rows = chunk(r)
        xr[rows, 0:LANES] = parts[rows, 0:LANES]
        xr[rows, LANES:2 * LANES] = bt[rows, :]
    first_modes = iota((CHUNK, LANES), 1) < RP
    for r in range(chunks):
        rows = chunk(r)
        out = jnp.dot(a[rows, :], xr[...], preferred_element_type=F32)
        img[rows, 0:LANES] = out[:, 0:LANES].astype(BF16)
        g = out[:, LANES:2 * LANES]
        y[rows, :] = g
        high, rest = split(g)
        img[rows, LANES:2 * LANES] = jnp.where(first_modes, high.astype(F32), rest.astype(F32)).astype(BF16)
    snd[...] = jnp.dot(send_hot[...], img[...], preferred_element_type=F32).astype(BF16)
    pair = exchange(0)

    to_all(evb, vsend, vrecv)
    around = [(i, j) for i in (-1, 0, 1) for j in (-1, 0, 1) if (i, j) != (0, 0)]
    for i, j in around:
        pltpu.make_async_remote_copy(
            src_ref=fcb.at[4], dst_ref=fcb.at[(1 - i) * 3 + 1 - j],
            send_sem=csend, recv_sem=crecv,
            device_id=(lax.rem(sub + i + ns, ns), lax.rem(load + j + nl, nl)),
            device_id_type=MESH,
        ).start()

    lane = iota((LANES, LANES), 1).astype(F32)
    for r in range(blocks):
        rows = pl.ds(r * LANES, LANES)
        pcol = jnp.transpose(jnp.broadcast_to(prow[:, r * LANES:(r + 1) * LANES], (LANES, LANES)))
        below = jnp.zeros((LANES, LANES), F32)
        for c in range(blocks):
            cols = pl.ds(c * LANES, LANES)
            own_hot[rows, cols] = hot(pcol == lane + float(spots + c * LANES))
            below = below + jnp.where(pcol > prow[:, c * LANES:(c + 1) * LANES], 1.0, 0.0)
        rank = jnp.broadcast_to(jnp.sum(below, axis=1, keepdims=True), (LANES, LANES))
        place = jnp.where(
            pcol < float(spots),
            rank,
            jnp.where(pcol >= float(2 * spots), rank - float(2 * quarter), -1.0),
        )
        for c in range(2 * quarter // LANES):
            recv_hot[rows, pl.ds(c * LANES, LANES)] = hot(place == lane + float(c * LANES))
    offset = iota(sel.shape, 1) - EDOF * iota(sel.shape, 0)
    sel[...] = hot((offset >= 0) & (offset < EDOF))

    block_at = iota((CHUNK, LANES), 1) >> 4
    for r in range(chunks):
        rows = chunk(r)
        mine = jnp.dot(own_hot[rows, :], img[...], preferred_element_type=F32)
        inner = mine[:, LANES:2 * LANES]
        inner = inner + pltpu.roll(inner, LANES - RP, 1)
        inner = jnp.where(first_modes, inner, 0.0)
        inner = inner + pltpu.roll(inner, RP, 1)
        g = y[rows, :] + inner
        high, rest = split(g)
        g = jnp.where(first_modes, high.astype(F32), rest.astype(F32))
        g = jnp.where(block_at < 2, g, 0.0)
        da[rows, :] = pltpu.roll(g, 4 * RP, 1)
        y[rows, :] = img[rows, 0:LANES].astype(F32) + mine[:, 0:LANES]

    for copy in pair:
        copy.wait_recv()
    upper = pl.ds(quarter, quarter)
    wide_lane = iota((quarter, LANES), 1)
    moved_part = jnp.where(wide_lane < 2 * RP, rcv[upper, LANES:2 * LANES].astype(F32), 0.0)
    rcv[upper, LANES:2 * LANES] = pltpu.roll(moved_part, 2 * RP, 1).astype(BF16)
    lower = pl.ds(0, quarter)
    rcv[lower, LANES:2 * LANES] = jnp.where(
        wide_lane < 2 * RP, rcv[lower, LANES:2 * LANES].astype(F32), 0.0
    ).astype(BF16)
    for r in range(chunks):
        rows = chunk(r)
        other = jnp.dot(recv_hot[rows, :], rcv[...], preferred_element_type=F32)
        y[rows, :] = y[rows, :] + other[:, 0:LANES]
        modes_image = (da[rows, :] + other[:, LANES:2 * LANES]).astype(BF16)
        hw[rows, 0:LANES] = modes_image
        hw[rows, LANES:2 * LANES] = modes_image

    entries = float(n * spots)

    def solve(it):
        settle(ag.at[it], grecv.at[it])
        solved = jnp.dot(
            cp[...], ag[it].reshape(n * RP, LANES), preferred_element_type=F32
        )
        cs = [solved[2 * d * RP:(2 * d + 1) * RP] + solved[(2 * d + 1) * RP:(2 * d + 2) * RP] for d in range(3)]
        mean = cs[2][modes:modes + 1] / entries
        step_size = damp[...] / jnp.sqrt(mean + EPSILON)
        return cs, step_size

    def advance(step_size, before, first):
        for r in range(chunks):
            rows = chunk(r)
            move = step_size * (before[rows, :] - jnp.dot(bt[rows, :], ck[...], preferred_element_type=F32))
            x[rows, :] = move if first else x[rows, :] + move

    for it in range(ITERS - 1):
        before = rhs if it == 0 else res.at[it - 1]
        if it == 0:
            for copy in near:
                copy.wait_recv()
        cs, step_size = solve(it)
        for d in range(3):
            high, rest = split(cs[d])
            for k in range(2):
                ckw[(2 * d + k) * RP:(2 * d + k + 1) * RP, :] = high
                ckw[LANES + (2 * d + k) * RP:LANES + (2 * d + k + 1) * RP, :] = rest
            if d == 2:
                ck[0:RP, :] = high
                ck[RP:2 * RP, :] = rest
        total = jnp.zeros((8, LANES), F32)
        for r in range(chunks):
            rows = chunk(r)
            left = before[rows, :] - step_size * (
                y[rows, :] - jnp.dot(hw[rows, :], ckw[...], preferred_element_type=F32)
            )
            res[it, rows, :] = left
            total = total + keep_parts(rows, left)
        gather_terms(it + 1, total)
        to_all(ag.at[it + 1], gsend.at[it + 1], grecv.at[it + 1])

        if it + 2 < ITERS:
            for r in range(chunks):
                rows = chunk(r)
                img[rows, 0:LANES] = jnp.dot(
                    a[rows, :], parts[:, 0:LANES], preferred_element_type=F32
                ).astype(BF16)
            snd1[...] = jnp.dot(
                send_hot[...], img[:, 0:LANES], preferred_element_type=F32
            ).astype(BF16)
            near = near + pair
            pair = exchange(it + 1)
            advance(step_size, before, it == 0)
            for r in range(chunks):
                rows = chunk(r)
                y[rows, :] = img[rows, 0:LANES].astype(F32) + jnp.dot(
                    own_hot[rows, :], img[:, 0:LANES], preferred_element_type=F32
                )
            if it == 0:
                settle(evb, vrecv)

                @pl.loop(0, n)
                def _(s):
                    column = evb[s] & (LANES - 1)
                    spot = (lax.rem(s, nl) - load) * LANES + column + MARGIN_C
                    colhot[:, pl.ds(pl.multiple_of(s * LANES, LANES), LANES)] = hot(
                        iota((2 * LANES, LANES), 0) == spot
                    )
            for copy in pair:
                copy.wait_recv()
            for r in range(chunks):
                rows = chunk(r)
                y[rows, :] = y[rows, :] + jnp.dot(
                    recv_hot[rows, :], rcv1[...], preferred_element_type=F32
                )
        else:
            advance(step_size, before, it == 0)

    last = res.at[ITERS - 2]
    for r in range(chunks):
        rows = chunk(r)
        xr[rows, 0:LANES] = x[rows, :].astype(BF16)
        xr[rows, LANES:2 * LANES] = parts[rows, 0:LANES]
    for copy in local[8:]:
        copy.wait()
    unknowns = rec.shape[0]
    for r in range(unknowns // CHUNK):
        rows = chunk(r)
        out = jnp.dot(rec[rows, :], xr[...], preferred_element_type=F32)
        da[rows, :] = base[rows, :].astype(F32) - out[:, 0:LANES]
        db[rows, :] = out[:, LANES:2 * LANES]
        g = jnp.dot(rec[rows, :], bt[...], preferred_element_type=F32)
        high, rest = split(g)
        rb[rows, :] = jnp.where((block_at & 1) == 0, high.astype(F32), rest.astype(F32)).astype(BF16)

    cs, step_size = solve(ITERS - 1)
    high, rest = split(cs[2])
    ck[0:RP, :] = high
    ck[RP:2 * RP, :] = rest
    ckw[0:RP, :] = high
    ckw[RP:2 * RP, :] = high
    ckw[2 * RP:3 * RP, :] = rest
    ckw[3 * RP:4 * RP, :] = rest
    for r in range(unknowns // CHUNK):
        rows = chunk(r)
        displaced = da[rows, :] - step_size * (
            db[rows, :] - jnp.dot(rb[rows, 0:4 * RP], ckw[0:4 * RP, :], preferred_element_type=F32)
        )
        high, rest = split(displaced * adj[rows, :].astype(F32))
        prod[rows, 0:LANES] = high
        prod[rows, LANES:2 * LANES] = rest

    both = jnp.dot(sel[...], prod[...], preferred_element_type=F32)
    grads = jnp.sum(
        jnp.transpose(both[:, 0:LANES] + both[:, LANES:2 * LANES]), axis=0, keepdims=True
    ) / math.sqrt(EDOF * LANES)
    egb[me] = grads
    to_all(egb, esend, erecv)

    advance(step_size, last, False)
    out_copy = pltpu.make_async_copy(x, x_h.at[0], lsem.at[11])
    out_copy.start()

    pltpu.make_async_copy(fcb.at[pl.ds(0, 8)], fcb.at[pl.ds(0, 8)], crecv).wait()
    classes = jnp.concatenate(
        [jnp.concatenate([fcb[3 * i + j] for j in range(3)], axis=1) for i in range(3)], axis=0
    )
    high_r, wide_c = 2 * 8, 2 * LANES
    classes = pltpu.roll(classes, 3 * 8 - (8 - MARGIN_R), 0)[0:high_r]
    classes = pltpu.roll(classes, 3 * LANES - (LANES - MARGIN_C), 1)[:, 0:wide_c]
    grid_row = iota((high_r, wide_c), 0) + (sub * 8 - MARGIN_R)
    grid_col = iota((high_r, wide_c), 1) + (load * LANES - MARGIN_C)
    inside = (grid_row >= 0) & (grid_row < ns * 8) & (grid_col >= 0) & (grid_col < nl * LANES)

    settle(egb, erecv)

    def place_rows(s, carry):
        here = iota((RP, LANES), 0) == (evb[s] >> 7) - (sub * 8 - MARGIN_R)
        high, rest = split(jnp.where(here, egb[s], 0.0))
        cols = pl.ds(pl.multiple_of(s * LANES, LANES), LANES)
        rowval[0:RP, cols] = high
        rowval[RP:2 * RP, cols] = rest
        return carry

    lax.fori_loop(0, n, place_rows, 0, unroll=8)
    sums = lax.dot_general(
        rowval[...], colhot[...], (((1,), (1,)), ((), ())), preferred_element_type=F32
    )
    field = sums[0:RP] + sums[RP:2 * RP]

    def moved(value, by_row, by_col):
        if by_row:
            value = pltpu.roll(value, (-by_row) % high_r, 0)
        if by_col:
            value = pltpu.roll(value, (-by_col) % wide_c, 1)
        return value

    for repeat in range(SMOOTH):
        field = jnp.where(inside, field, 0.0)
        up, down = moved(field, 1, 0), moved(field, -1, 0)
        along_rows = up + down - 2.0 * field
        along_cols = moved(field, 0, 1) + moved(field, 0, -1) - 2.0 * field
        diag_main = moved(up, 0, 1) + moved(down, 0, -1) - 2.0 * field
        diag_anti = moved(up, 0, -1) + moved(down, 0, 1) - 2.0 * field
        chosen = jnp.where(
            classes == 0,
            along_rows,
            jnp.where(classes == 1, along_cols, jnp.where(classes == 2, diag_main, diag_anti)),
        )
        field = field + FIBRE_RATE * chosen + ISO_RATE * (along_rows + along_cols)
    fout[...] = moved(field, MARGIN_R, MARGIN_C)[0:8, 0:LANES]
    field_copy = pltpu.make_async_copy(fout, f_h, lsem.at[12])
    field_copy.start()

    for copy in near + pair:
        copy.wait_send()
    for it in range(ITERS):
        settle(ag.at[it], gsend.at[it])
    settle(evb, vsend)
    settle(egb, esend)
    pltpu.make_async_copy(fcb.at[pl.ds(0, 8)], fcb.at[pl.ds(0, 8)], csend).wait()
    out_copy.wait()
    field_copy.wait()


def on_device(ns, nl, *args):
    (dual_ops, dual_rhs, partner, coarse_basis, coarse_inverse, damping,
     recovery, base_disp, adjoint, elem_voxel, fibre_class) = args
    n = ns * nl
    spots, columns = dual_rhs.shape[1:]
    modes = coarse_basis.shape[1]
    unknowns = recovery.shape[1]
    elements = elem_voxel.shape[1]
    half = spots // 2
    dma = pltpu.SemaphoreType.DMA
    scratch = [
        pltpu.VMEM((spots, spots), BF16),
        pltpu.VMEM((spots, columns), F32),
        pltpu.VMEM((1, spots), I32),
        pltpu.VMEM((modes, spots), BF16),
        pltpu.VMEM(coarse_inverse.shape, F32),
        pltpu.VMEM((1, columns), F32),
        pltpu.VMEM((unknowns, spots), BF16),
        pltpu.VMEM((unknowns, columns), BF16),
        pltpu.VMEM((unknowns, columns), BF16),
        pltpu.VMEM((n, 1, elements), I32),
        pltpu.VMEM((9,) + fibre_class.shape, I32),
        pltpu.VMEM((spots, spots), BF16),
        pltpu.VMEM((spots, half), BF16),
        pltpu.VMEM((half, spots), BF16),
        pltpu.VMEM((spots, columns), F32),
        pltpu.VMEM((spots, 2 * columns), BF16),
        pltpu.VMEM((spots, 2 * columns), BF16),
        pltpu.VMEM((spots, columns), F32),
        pltpu.VMEM((ITERS - 1, spots, columns), F32),
        pltpu.VMEM((spots, 2 * columns), BF16),
        pltpu.VMEM((half, 2 * columns), BF16),
        pltpu.VMEM((half, 2 * columns), BF16),
        pltpu.VMEM((half, columns), BF16),
        pltpu.VMEM((half, columns), BF16),
        pltpu.VMEM((LANES, spots), F32),
        pltpu.VMEM((spots, LANES), BF16),
        pltpu.VMEM((RP, spots), BF16),
        pltpu.VMEM((GROUP * modes, GROUP * RP), BF16),
        pltpu.VMEM((2 * RP, n * RP), F32),
        pltpu.VMEM((6 * RP, n * RP), BF16),
        pltpu.VMEM((ITERS, n, RP, columns), BF16),
        pltpu.VMEM((LANES, columns), BF16),
        pltpu.VMEM((spots, 2 * LANES), BF16),
        pltpu.VMEM((2 * LANES, columns), BF16),
        pltpu.VMEM((unknowns, LANES), BF16),
        pltpu.VMEM((unknowns, columns), F32),
        pltpu.VMEM((unknowns, columns), F32),
        pltpu.VMEM((unknowns, 2 * columns), BF16),
        pltpu.VMEM((elements, unknowns), BF16),
        pltpu.VMEM((n, 1, elements), F32),
        pltpu.VMEM((2 * LANES, n * elements), BF16),
        pltpu.VMEM((2 * RP, n * elements), BF16),
        pltpu.VMEM(fibre_class.shape, F32),
        dma((13,)),
        dma((ITERS - 1, 2)),
        dma((ITERS - 1, 2)),
        dma((ITERS,)),
        dma((ITERS,)),
        dma((2,)),
        dma((2,)),
        dma, dma, dma, dma, dma, dma,
    ]
    anywhere = pl.BlockSpec(memory_space=pl.ANY)
    multipliers, field = pl.pallas_call(
        functools.partial(kernel, ns, nl),
        out_shape=(
            jax.ShapeDtypeStruct((1, spots, columns), F32),
            jax.ShapeDtypeStruct(fibre_class.shape, F32),
        ),
        in_specs=[anywhere] * 11,
        out_specs=(anywhere, anywhere),
        scratch_shapes=scratch,
        compiler_params=pltpu.CompilerParams(
            collective_id=0, has_side_effects=True, vmem_limit_bytes=62 * 1024 * 1024
        ),
    )(
        dual_ops, dual_rhs, partner, coarse_basis, coarse_inverse,
        damping.reshape(1, columns), recovery, base_disp, adjoint, elem_voxel, fibre_class,
    )
    return multipliers, field


def solution(mesh):
    ns, nl = mesh.shape["sub"], mesh.shape["load"]
    placed = (
        P(("sub", "load"), None, None),
        P(("sub", "load"), None, None),
        P(("sub", "load"), None),
        P(("sub", "load"), None, None),
        P(("sub", "load"), None),
        P(),
        P(("sub", "load"), None, None),
        P(("sub", "load"), None, None),
        P(("sub", "load"), None, None),
        P(("sub", "load"), None),
        P("sub", "load"),
    )
    return jax.shard_map(
        functools.partial(on_device, ns, nl),
        mesh=mesh,
        in_specs=placed,
        out_specs=(P(("sub", "load"), None, None), P("sub", "load")),
        check_vma=False,
    )
```

time: 51.6 us -> 39 us (0.76)
  Pallas kernels: 47.6 us -> 35 us
    pallas_call x1, Pallas kernels: 47.6 us -> 35 us  [on_device(): pl.pallas_call(functools.partial(kernel, ns, nl), out_shape=(jax.ShapeDty...]
where the time goes in v1:
time: 39 us; the launch traced here: 38.8 us
  Pallas kernels  35 us (90%)
  local copies, waits for them, and re-layouts  3.13 us (8%)
  between operations  0.64 us (2%)
    pallas_call x1, Pallas kernels, on_device(): pl.pallas_call(functools.partial(kernel, ns, nl), out_shape=(jax.ShapeDty...  35 us
    unnamed x2, local copies, waits for them, and re-layouts  3.13 us

profile of v1, /device:TPU:0, one launch (start us, length us, event | category | flops | bytes accessed | tf_op | source)
XLA Modules:
  0.0 38.8 jit_solution(18387613671182541135)
XLA Ops:
  0.6 35.0 %shard_map.122 = (f32[1,1024,128]{2,1,0:T(8,128)}, f32[8,128]{1,0:T(8,128)}) custom-call(bf16[1,1024,1024]{2,1,0:T(8,128)(2,1)} %a_h.1, f32[1,1024,128]{2,1,0:T(8,128)} %rhs_h.1, s32[1,1024]{1,0:T(1,128)} %par_h.1, bf16[1,12,1024]{2,1,0:T(8,128)(2,1)} %b_h.1, f32[12,384]{1,0:T(8,128)} %ci_h.1, f32[1,128]{1,0:T(1,128)} %bitcast.1, ...), custom_call_target="tpu_custom_call" | custom-call | tf_op jit(solution)/shard_map/pallas_call | solution.py:547
  35.6 1.9 %copy.15 = f32[1,1024,128]{2,1,0:T(8,128)} copy(f32[1,1024,128]{2,1,0:T(8,128)} %get-tuple-element.4) | data formatting | bytes 1048576
  37.5 1.3 %copy.16 = f32[8,128]{1,0:T(8,128)} copy(f32[8,128]{1,0:T(8,128)} %get-tuple-element.5) | data formatting | bytes 8192

commit v2 on v0

v2 whole, which is shorter than its diff:
```python
import functools
import math

import jax
import jax.numpy as jnp
from jax import lax
from jax.experimental import pallas as pl
from jax.experimental.pallas import tpu as pltpu
from jax.sharding import PartitionSpec as P

EDOF = 12
ITERS = 3
SMOOTH = 2
FIBRE_RATE = 0.3
ISO_RATE = 0.05
EPSILON = 1e-06

F32 = jnp.float32
BF16 = jnp.bfloat16
I32 = jnp.int32
MESH = pl.DeviceIdType.MESH
LANES = 128
CHUNK = 256
RP = 16
GROUP = 32
MARGIN_R = 4
MARGIN_C = 64


def iota(shape, dim):
    return lax.broadcasted_iota(I32, shape, dim)


def hot(cond):
    return jnp.where(cond, 1.0, 0.0).astype(BF16)


def split(value):
    high = value.astype(BF16)
    return high, (value - high.astype(F32)).astype(BF16)


def kernel(
    ns, nl,
    a_h, rhs_h, par_h, b_h, ci_h, damp_h, rec_h, base_h, adj_h, ev_h, fc_h,
    x_o, f_o,
    a, rhs, par, b, ci, damp, rec, base, adj, evb, fcb,
    own_hot, recv_hot, send_hot, x, xb, img, tmp, res, parts, snd, rcv,
    bwide, bt, bp, spread, cpf, cp, ag, ck, prod, sel, egb, colhot, rowhot, rowval,
    lsem, nsend, nrecv, gsend, grecv, vsend, vrecv, csend, crecv, esend, erecv,
):
    n = ns * nl
    spots = a.shape[0]
    quarter = spots // 4
    modes = b.shape[0]
    sub, load = lax.axis_index("sub"), lax.axis_index("load")
    me = sub * nl + load

    def dev(p):
        return (lax.div(p, nl), lax.rem(p, nl))

    def peer(k):
        return lax.rem(me + k, n)

    local = [
        pltpu.make_async_copy(src, dst, lsem.at[i])
        for i, (src, dst) in enumerate((
            (par_h, par),
            (b_h.at[0], b),
            (ci_h, ci),
            (ev_h, evb.at[me]),
            (fc_h, fcb.at[4]),
            (damp_h, damp),
            (a_h.at[0], a),
            (rhs_h.at[0], rhs),
            (rec_h.at[0], rec),
            (base_h.at[0], base),
            (adj_h.at[0], adj),
        ))
    ]
    for i in (1, 7, 0, 2, 5, 6, 3, 4):
        local[i].start()

    barrier = pltpu.get_barrier_semaphore()

    def each_peer(act):
        @pl.loop(0, ns)
        def _(i):
            far = jnp.where(2 * sub < ns, ns - 1 - i, i)
            for j in range(nl):
                across = jnp.where(2 * load < nl, nl - 1 - j, j)

                @pl.when(far * nl + across != me)
                def _():
                    act((far, across))

    each_peer(lambda to: pl.semaphore_signal(barrier, inc=1, device_id=to, device_id_type=MESH))

    def to_all(ref, send, recv):
        each_peer(lambda to: pltpu.make_async_remote_copy(
            src_ref=ref.at[me], dst_ref=ref.at[me], send_sem=send, recv_sem=recv,
            device_id=to, device_id_type=MESH,
        ).start())

    def settle(ref, sem):
        part = ref.at[pl.ds(0, n - 1)]
        pltpu.make_async_copy(part, part, sem).wait()

    blocks = spots // LANES
    local[1].wait()
    bwide[...] = jnp.zeros_like(bwide)
    basis = b[...].astype(F32)
    bwide[0:modes, :] = basis
    bwide[RP:RP + modes, :] = basis
    bp[...] = bwide[0:RP, :].astype(BF16)
    local[7].wait()

    def keep_parts(rows, left, total):
        res[rows, :] = left
        high, rest = split(left)
        parts[rows, 0:LANES] = high
        parts[rows, LANES:2 * LANES] = rest
        return total + jnp.sum((left * left).reshape(CHUNK // 8, 8, LANES), axis=0)

    def send_terms(it, total):
        both = jnp.dot(bp[...], parts[...], preferred_element_type=F32)
        terms = both[:, 0:LANES] + both[:, LANES:2 * LANES]
        squares = jnp.sum(total, axis=0, keepdims=True)
        high, rest = split(squares)
        row = iota((RP, LANES), 0)
        terms = jnp.where(row == modes, high.astype(F32), terms)
        terms = jnp.where(row == modes + 1, rest.astype(F32), terms)
        ag[it, me] = terms.astype(BF16)
        if it == 0:
            pl.semaphore_wait(barrier, n - 1)
        to_all(ag.at[it], gsend.at[it], grecv.at[it])

    entries = float(n * spots)
    near = []
    for it in range(ITERS):
        total = jnp.zeros((8, LANES), F32)
        if it == 0:
            for r in range(spots // CHUNK):
                rows = pl.ds(r * CHUNK, CHUNK)
                total = keep_parts(rows, rhs[rows, :], total)
            send_terms(it, total)
        else:
            for r in range(spots // CHUNK):
                rows = pl.ds(r * CHUNK, CHUNK)
                img[rows, :] = jnp.dot(a[rows, :], xb[...], preferred_element_type=F32).astype(BF16)
            for side, step in enumerate((1, n - 1)):
                half = pl.ds(side * quarter, quarter)
                snd[it, half] = jnp.dot(
                    send_hot[half, :], img[...], preferred_element_type=F32
                ).astype(BF16)
                copy = pltpu.make_async_remote_copy(
                    src_ref=snd.at[it, half], dst_ref=rcv.at[it, half],
                    send_sem=nsend.at[it, side], recv_sem=nrecv.at[it, side],
                    device_id=dev(peer(step)), device_id_type=MESH,
                )
                copy.start()
                near.append(copy)
            for r in range(spots // CHUNK):
                rows = pl.ds(r * CHUNK, CHUNK)
                tmp[rows, :] = rhs[rows, :] - (img[rows, :].astype(F32) + jnp.dot(
                    own_hot[rows, :], img[...], preferred_element_type=F32
                ))
            near[-2].wait_recv()
            near[-1].wait_recv()
            for r in range(spots // CHUNK):
                rows = pl.ds(r * CHUNK, CHUNK)
                left = tmp[rows, :] - jnp.dot(
                    recv_hot[rows, :], rcv[it], preferred_element_type=F32
                )
                total = keep_parts(rows, left, total)
            send_terms(it, total)

        if it == 0:
            local[3].wait()
            local[4].wait()
            local[5].wait()
            local[6].wait()
            for copy in local[8:]:
                copy.start()
        if it == 0:
            to_all(evb, vsend, vrecv)
            around = [(i, j) for i in (-1, 0, 1) for j in (-1, 0, 1) if (i, j) != (0, 0)]
            for i, j in around:
                pltpu.make_async_remote_copy(
                    src_ref=fcb.at[4], dst_ref=fcb.at[(1 - i) * 3 + 1 - j],
                    send_sem=csend, recv_sem=crecv,
                    device_id=(lax.rem(sub + i + ns, ns), lax.rem(load + j + nl, nl)),
                    device_id_type=MESH,
                ).start()
        if it == 0:
            for r in range(blocks):
                bt[pl.ds(r * LANES, LANES), :] = jnp.transpose(
                    bwide[:, r * LANES:(r + 1) * LANES]
                ).astype(BF16)
            ck[...] = jnp.zeros_like(ck)
            local[2].wait()
            deep, broad = spread.shape
            at_col = iota((deep, broad), 1)
            within = at_col & (RP - 1)
            from_row = (at_col >> 4) * modes + within
            spread[...] = hot((iota((deep, broad), 0) == from_row) & (within < modes))
            cpf[...] = jnp.zeros_like(cpf)
            for g in range(n // GROUP):
                high, rest = split(ci[:, g * deep:(g + 1) * deep])
                cols = pl.ds(g * broad, broad)
                cpf[0:modes, cols] = jnp.dot(high, spread[...], preferred_element_type=F32)
                cpf[RP:RP + modes, cols] = jnp.dot(rest, spread[...], preferred_element_type=F32)
                mode = iota((1, broad), 1) & (RP - 1)
                cpf[modes:modes + 1, cols] = jnp.where((mode == modes) | (mode == modes + 1), 1.0, 0.0)
            cp[...] = cpf[...].astype(BF16)
            offset = iota(sel.shape, 1) - EDOF * iota(sel.shape, 0)
            sel[...] = hot((offset >= 0) & (offset < EDOF))

            local[0].wait()
            prow = par[...].astype(F32)
            lane = iota((LANES, LANES), 1).astype(F32)
            for r in range(blocks):
                rows = pl.ds(r * LANES, LANES)
                pcol = jnp.transpose(jnp.broadcast_to(prow[:, r * LANES:(r + 1) * LANES], (LANES, LANES)))
                below = jnp.zeros((LANES, LANES), F32)
                for c in range(blocks):
                    cols = pl.ds(c * LANES, LANES)
                    own_hot[rows, cols] = hot(pcol == lane + float(spots + c * LANES))
                    below = below + jnp.where(pcol > prow[:, c * LANES:(c + 1) * LANES], 1.0, 0.0)
                rank = jnp.broadcast_to(jnp.sum(below, axis=1, keepdims=True), (LANES, LANES))
                place = jnp.where(
                    pcol < float(spots),
                    rank,
                    jnp.where(pcol >= float(2 * spots), rank - float(2 * quarter), -1.0),
                )
                for c in range(2 * quarter // LANES):
                    recv_hot[rows, pl.ds(c * LANES, LANES)] = hot(place == lane + float(c * LANES))
            to_next = jnp.where(prow >= float(2 * spots), 1.0, 0.0)
            to_prev = jnp.where(prow < float(spots), 1.0, 0.0)
            count = jnp.where(iota((8, spots), 0) == 0, to_next, to_prev)
            wide = iota((8, spots), 1)
            shift = 1
            while shift < spots:
                count = count + jnp.where(wide >= shift, pltpu.roll(count, shift, 1), 0.0)
                shift *= 2
            slot = jnp.where(
                to_next > 0.5,
                count[0:1] - 1.0,
                jnp.where(to_prev > 0.5, count[1:2] - 1.0 + float(quarter), -1.0),
            )
            for r in range(2 * quarter // LANES):
                at = (iota((LANES, spots), 0) + r * LANES).astype(F32)
                send_hot[pl.ds(r * LANES, LANES), :] = hot(slot == at)

        if it == 1:
            settle(evb, vrecv)

            @pl.loop(0, n)
            def _(s):
                column = evb[s] & (LANES - 1)
                spot = (lax.rem(s, nl) - load) * LANES + column + MARGIN_C
                cols = pl.ds(pl.multiple_of(s * LANES, LANES), LANES)
                spots_at = jnp.transpose(jnp.broadcast_to(spot.astype(F32), (LANES, LANES)))
                here = iota((LANES, LANES), 1).astype(F32)
                colhot[cols, 0:LANES] = hot(spots_at == here)
                colhot[cols, LANES:2 * LANES] = hot(spots_at == here + float(LANES))
                rowhot[:, cols] = hot(iota((RP, LANES), 0) == (evb[s] >> 7) - (sub * 8 - MARGIN_R))

        settle(ag.at[it], grecv.at[it])
        solved = jnp.dot(
            cp[...], ag[it].reshape(n * RP, LANES), preferred_element_type=F32
        )
        correction = solved[0:RP] + solved[RP:2 * RP]
        mean = correction[modes:modes + 1] / entries
        step_size = damp[...] / jnp.sqrt(mean + EPSILON)
        high, rest = split(correction)
        ck[0:RP, :] = high
        ck[RP:2 * RP, :] = rest

        @pl.loop(0, spots // CHUNK, unroll=True)
        def _(r):
            rows = pl.ds(pl.multiple_of(r * CHUNK, CHUNK), CHUNK)
            projected = res[rows, :] - jnp.dot(bt[rows, :], ck[...], preferred_element_type=F32)
            new = step_size * projected if it == 0 else x[rows, :] + step_size * projected
            if it == ITERS - 1:
                x_o[0, rows, :] = new
            else:
                x[rows, :] = new
            xb[rows, :] = new.astype(BF16)

    for copy in local[8:]:
        copy.wait()
    unknowns = rec.shape[0]

    @pl.loop(0, unknowns // CHUNK, unroll=True)
    def _(r):
        rows = pl.ds(pl.multiple_of(r * CHUNK, CHUNK), CHUNK)
        displaced = base[rows, :].astype(F32) - jnp.dot(
            rec[rows, :], xb[...], preferred_element_type=F32
        )
        high, rest = split(displaced * adj[rows, :].astype(F32))
        prod[rows, 0:LANES] = high
        prod[rows, LANES:2 * LANES] = rest

    both = jnp.dot(sel[...], prod[...], preferred_element_type=F32)
    grads = jnp.sum(
        jnp.transpose(both[:, 0:LANES] + both[:, LANES:2 * LANES]), axis=0, keepdims=True
    ) / math.sqrt(EDOF * LANES)
    egb[me] = grads
    to_all(egb, esend, erecv)

    pltpu.make_async_copy(fcb.at[pl.ds(0, 8)], fcb.at[pl.ds(0, 8)], crecv).wait()
    classes = jnp.concatenate(
        [jnp.concatenate([fcb[3 * i + j] for j in range(3)], axis=1) for i in range(3)], axis=0
    )
    high_r, wide_c = 2 * 8, 2 * LANES
    classes = pltpu.roll(classes, 3 * 8 - (8 - MARGIN_R), 0)[0:high_r]
    classes = pltpu.roll(classes, 3 * LANES - (LANES - MARGIN_C), 1)[:, 0:wide_c]
    grid_row = iota((high_r, wide_c), 0) + (sub * 8 - MARGIN_R)
    grid_col = iota((high_r, wide_c), 1) + (load * LANES - MARGIN_C)
    inside = (grid_row >= 0) & (grid_row < ns * 8) & (grid_col >= 0) & (grid_col < nl * LANES)

    settle(egb, erecv)

    def place_rows(s, carry):
        cols = pl.ds(pl.multiple_of(s * LANES, LANES), LANES)
        here = rowhot[:, cols]
        high, rest = split(jnp.broadcast_to(egb[s], (RP, LANES)))
        rowval[0:RP, cols] = high * here
        rowval[RP:2 * RP, cols] = rest * here
        return carry

    lax.fori_loop(0, n, place_rows, 0, unroll=min(n, 32))
    sums = jnp.dot(rowval[...], colhot[...], preferred_element_type=F32)
    field = sums[0:RP] + sums[RP:2 * RP]

    def moved(value, by_row, by_col):
        if by_row:
            value = pltpu.roll(value, (-by_row) % high_r, 0)
        if by_col:
            value = pltpu.roll(value, (-by_col) % wide_c, 1)
        return value

    for repeat in range(SMOOTH):
        field = jnp.where(inside, field, 0.0)
        up, down = moved(field, 1, 0), moved(field, -1, 0)
        along_rows = up + down - 2.0 * field
        along_cols = moved(field, 0, 1) + moved(field, 0, -1) - 2.0 * field
        diag_main = moved(up, 0, 1) + moved(down, 0, -1) - 2.0 * field
        diag_anti = moved(up, 0, -1) + moved(down, 0, 1) - 2.0 * field
        chosen = jnp.where(
            classes == 0,
            along_rows,
            jnp.where(classes == 1, along_cols, jnp.where(classes == 2, diag_main, diag_anti)),
        )
        field = field + FIBRE_RATE * chosen + ISO_RATE * (along_rows + along_cols)
    f_o[...] = moved(field, MARGIN_R, MARGIN_C)[0:8, 0:LANES]

    for copy in near:
        copy.wait_send()
    for it in range(ITERS):
        settle(ag.at[it], gsend.at[it])
    settle(evb, vsend)
    settle(egb, esend)
    pltpu.make_async_copy(fcb.at[pl.ds(0, 8)], fcb.at[pl.ds(0, 8)], csend).wait()


def deliver(x, field, x_h, f_h, sem):
    copies = [
        pltpu.make_async_copy(x, x_h, sem.at[0]),
        pltpu.make_async_copy(field, f_h, sem.at[1]),
    ]
    for copy in copies:
        copy.start()
    for copy in copies:
        copy.wait()


def on_device(ns, nl, *args):
    (dual_ops, dual_rhs, partner, coarse_basis, coarse_inverse, damping,
     recovery, base_disp, adjoint, elem_voxel, fibre_class) = args
    n = ns * nl
    spots, columns = dual_rhs.shape[1:]
    modes = coarse_basis.shape[1]
    unknowns = recovery.shape[1]
    elements = elem_voxel.shape[1]
    half = spots // 2
    dma = pltpu.SemaphoreType.DMA
    scratch = [
        pltpu.VMEM((spots, spots), BF16),
        pltpu.VMEM((spots, columns), F32),
        pltpu.VMEM((1, spots), I32),
        pltpu.VMEM((modes, spots), BF16),
        pltpu.VMEM(coarse_inverse.shape, F32),
        pltpu.VMEM((1, columns), F32),
        pltpu.VMEM((unknowns, spots), BF16),
        pltpu.VMEM((unknowns, columns), BF16),
        pltpu.VMEM((unknowns, columns), BF16),
        pltpu.VMEM((n, 1, elements), I32),
        pltpu.VMEM((9,) + fibre_class.shape, I32),
        pltpu.VMEM((spots, spots), BF16),
        pltpu.VMEM((spots, half), BF16),
        pltpu.VMEM((half, spots), BF16),
        pltpu.VMEM((spots, columns), F32),
        pltpu.VMEM((spots, columns), BF16),
        pltpu.VMEM((spots, columns), BF16),
        pltpu.VMEM((spots, columns), F32),
        pltpu.VMEM((spots, columns), F32),
        pltpu.VMEM((spots, 2 * columns), BF16),
        pltpu.VMEM((ITERS, half, columns), BF16),
        pltpu.VMEM((ITERS, half, columns), BF16),
        pltpu.VMEM((LANES, spots), F32),
        pltpu.VMEM((spots, LANES), BF16),
        pltpu.VMEM((RP, spots), BF16),
        pltpu.VMEM((GROUP * modes, GROUP * RP), BF16),
        pltpu.VMEM((2 * RP, n * RP), F32),
        pltpu.VMEM((2 * RP, n * RP), BF16),
        pltpu.VMEM((ITERS, n, RP, columns), BF16),
        pltpu.VMEM((LANES, columns), BF16),
        pltpu.VMEM((unknowns, 2 * columns), BF16),
        pltpu.VMEM((elements, unknowns), BF16),
        pltpu.VMEM((n, 1, elements), F32),
        pltpu.VMEM((n * elements, 2 * LANES), BF16),
        pltpu.VMEM((RP, n * elements), BF16),
        pltpu.VMEM((2 * RP, n * elements), BF16),
        dma((11,)),
        dma((ITERS, 2)),
        dma((ITERS, 2)),
        dma((ITERS,)),
        dma((ITERS,)),
        dma, dma, dma, dma, dma, dma,
    ]
    anywhere = pl.BlockSpec(memory_space=pl.ANY)
    held = pl.BlockSpec(memory_space=pltpu.VMEM)
    multipliers, field = pl.pallas_call(
        functools.partial(kernel, ns, nl),
        out_shape=(
            pltpu.VMEM((1, spots, columns), F32),
            pltpu.VMEM(fibre_class.shape, F32),
        ),
        in_specs=[anywhere] * 11,
        out_specs=(held, held),
        scratch_shapes=scratch,
        compiler_params=pltpu.CompilerParams(
            collective_id=0, has_side_effects=True, vmem_limit_bytes=62 * 1024 * 1024
        ),
    )(
        dual_ops, dual_rhs, partner, coarse_basis, coarse_inverse,
        damping.reshape(1, columns), recovery, base_disp, adjoint, elem_voxel, fibre_class,
    )
    return pl.pallas_call(
        deliver,
        out_shape=(
            jax.ShapeDtypeStruct((1, spots, columns), F32),
            jax.ShapeDtypeStruct(fibre_class.shape, F32),
        ),
        in_specs=[anywhere, anywhere],
        out_specs=(anywhere, anywhere),
        scratch_shapes=[dma((2,))],
    )(pltpu.with_memory_space_constraint(multipliers, pltpu.VMEM), pltpu.with_memory_space_constraint(field, pltpu.VMEM))


def solution(mesh):
    ns, nl = mesh.shape["sub"], mesh.shape["load"]
    placed = (
        P(("sub", "load"), None, None),
        P(("sub", "load"), None, None),
        P(("sub", "load"), None),
        P(("sub", "load"), None, None),
        P(("sub", "load"), None),
        P(),
        P(("sub", "load"), None, None),
        P(("sub", "load"), None, None),
        P(("sub", "load"), None, None),
        P(("sub", "load"), None),
        P("sub", "load"),
    )
    return jax.shard_map(
        functools.partial(on_device, ns, nl),
        mesh=mesh,
        in_specs=placed,
        out_specs=(P(("sub", "load"), None, None), P("sub", "load")),
        check_vma=False,
    )
```

time: 51.6 us -> 42.4 us (0.82)
  Pallas kernels: 47.6 us -> 41.6 us
  local copies, waits for them, and re-layouts: 3.13 us -> 0 us
    pallas_call x1 -> x2, Pallas kernels: 47.6 us -> 41.6 us  [the longest x1 40.7 us: on_device(): pl.pallas_call(functools.partial(kernel, ns, nl), out_shape=(pltpu.VMEM((...]
    unnamed x2 -> x0, local copies, waits for them, and re-layouts: 3.13 us -> none
where the time goes in v2:
time: 42.4 us; the launch traced here: 42.2 us
  Pallas kernels  41.6 us (98%)
  between operations  0.64 us (2%)
    pallas_call x1, Pallas kernels, on_device(): pl.pallas_call(functools.partial(kernel, ns, nl), out_shape=(pltpu.VMEM((...  40.7 us

profile of v2, /device:TPU:0, one launch (start us, length us, event | category | flops | bytes accessed | tf_op | source)
XLA Modules:
  0.0 42.2 jit_solution(13745915012689233975)
XLA Ops:
  0.6 40.7 %shard_map.122 = (f32[1,1024,128]{2,1,0:T(8,128)S(1)}, f32[8,128]{1,0:T(8,128)S(1)}) custom-call(bf16[1,1024,1024]{2,1,0:T(8,128)(2,1)} %a_h.1, f32[1,1024,128]{2,1,0:T(8,128)} %rhs_h.1, s32[1,1024]{1,0:T(1,128)} %par_h.1, bf16[1,12,1024]{2,1,0:T(8,128)(2,1)} %b_h.1, f32[12,384]{1,0:T(8,128)} %ci_h.1, f32[1,128]{1,0:T(1,128)} %bitcast.1, ...), custom_call_target="tpu_custom_call" | custom-call | tf_op jit(solution)/shard_map/pallas_call | solution.py:435
  41.4 0.8 %shard_map.123 = (f32[1,1024,128]{2,1,0:T(8,128)}, f32[8,128]{1,0:T(8,128)}) custom-call(f32[1,1024,128]{2,1,0:T(8,128)S(1)} %get-tuple-element.4.x, f32[8,128]{1,0:T(8,128)S(1)} %get-tuple-element.5.field), custom_call_target="tpu_custom_call" | custom-call | tf_op jit(solution)/shard_map/pallas_call | solution.py:451
